TPU v7x, 32 devices: a whole 2x2x4 slice. The times are simulated.
32 devices in a mesh: dp: 8 (over y, x, core), tensor: 4 (over z).
Axes of the slice: x: 2, y: 2, z: 4, core: 2. Of those that a mesh axis runs over, the one named last changes fastest.
Arguments:
- hidden_in: bfloat16 [32, 512, 768], P('dp'), may hold values from -6 to 6
- out_grad: bfloat16 [32, 512, 768], P('dp'), may hold values from -3 to 3
- segment_ids: int32 [32, 512], P('dp'), may hold values from 0 to 7, never falling along the last dimension, each value on 1 to 256 neighbouring positions
- step_count: int32 [1], replicated, may hold values from 1 to 199999
- qkv_state: float32 [3, 768, 3, 768], P(None, 'dp', None, 'tensor'), as said below
- qv_bias_state: float32 [3, 2, 12, 64], P(None, None, 'tensor', 'dp'), as said below
- out_state: float32 [3, 768, 768], P(None, 'tensor', 'dp'), as said below
- up_state: float32 [3, 768, 3072], P(None, 'dp', 'tensor'), as said below
- up_bias_state: float32 [3, 24, 128], P(None, 'tensor', 'dp'), as said below
- down_state: float32 [3, 3072, 768], P(None, 'tensor', 'dp'), as said below
- vector_state: float32 [3, 6, 768], P(None, None, 'dp'), as said below
Outputs:
- hidden_out: bfloat16 [32, 512, 768], P('dp')
- grad_in: bfloat16 [32, 512, 768], P('dp')
- grad_qkv: float32 [768, 3, 768], P('dp', None, 'tensor')
- grad_qv_bias: float32 [2, 12, 64], P(None, 'tensor', 'dp')
- grad_out: float32 [768, 768], P('tensor', 'dp')
- grad_up: float32 [768, 3072], P('dp', 'tensor')
- grad_up_bias: float32 [24, 128], P('tensor', 'dp')
- grad_down: float32 [3072, 768], P('tensor', 'dp')
- grad_vectors: float32 [6, 768], P(None, 'dp')
- new_qkv_state: float32 [2, 768, 3, 768], P(None, 'dp', None, 'tensor')
- new_qv_bias_state: float32 [2, 2, 12, 64], P(None, None, 'tensor', 'dp')
- new_out_state: float32 [2, 768, 768], P(None, 'tensor', 'dp')
- new_up_state: float32 [2, 768, 3072], P(None, 'dp', 'tensor')
- new_up_bias_state: float32 [2, 24, 128], P(None, 'tensor', 'dp')
- new_down_state: float32 [2, 3072, 768], P(None, 'tensor', 'dp')
- new_vector_state: float32 [2, 6, 768], P(None, None, 'dp')
- plan: float32 [3], replicated
Inputs may be any that keep to these rules, and one draw needn't show every extreme that they name: `segment_ids`: within each packed row the fragment numbers never fall; a token attends exactly to the tokens of its own row with the same number. `qkv_state`: index 2 (second moments) is positive. `qv_bias_state`: index 2 (second moments) is positive. `out_state`: index 2 (second moments) is positive. `up_state`: index 2 (second moments) is positive. `up_bias_state`: index 2 (second moments) is positive. `down_state`: index 2 (second moments) is positive. `vector_state`: index 2 (second moments) is positive.
All inputs are finite; a program needn't handle non-finite values.
Results may differ from a plain program's by a relative error of at most 0.023.
The roundings to bfloat16 on the way count: a program that leaves them out, or rounds other values in their place, can miss the bound.
Values may be sent and summed in bfloat16 or wider, within the bound.
No kernel may reach another device: no remote copies, remote signals or barrier semaphores. Data moves between devices by JAX's collectives and lax.ppermute only.
A program may use at most 192 MiB of HBM per device.

v0:
```python
import math
import jax
import jax.numpy as jnp
from jax import lax
from jax.sharding import PartitionSpec as P

HD = 64
norm_eps = 1e-05
beta_first = 0.9
beta_second = 0.999
warm_steps = 10000.0
total_steps = 200000.0


def layer_norm(value, gain, shift):
    center = value - jnp.mean(value, axis=-1, keepdims=True)
    spread = jnp.mean(center * center, axis=-1, keepdims=True)
    return center * lax.rsqrt(spread + norm_eps) * gain + shift


def gelu_exact(value):
    return 0.5 * value * (1.0 + lax.erf(value * 0.7071067811865476))


def scores_of(query, key_rows, segments):
    raw = jnp.einsum(
        "bqhd,bkhd->bhqk", query, key_rows, preferred_element_type=jnp.float32
    ) * HD ** (-0.5)
    same = segments[:, :, None] == segments[:, None, :]
    return jnp.where(same[:, None], raw, -1e30)


def contract_rows(left, right):
    return lax.dot_general(
        left, right, (((0,), (0,)), ((), ())), preferred_element_type=jnp.float32
    )


def contract_cols(left, right):
    return lax.dot_general(
        left, right, (((1,), (1,)), ((), ())), preferred_element_type=jnp.float32
    )


def moment_update(state, grad):
    moment_one = beta_first * state[1] + (1.0 - beta_first) * grad
    moment_two = beta_second * state[2] + (1.0 - beta_second) * grad * grad
    return jnp.stack([moment_one, moment_two])


def body(
    hidden_in,
    out_grad,
    segment_ids,
    step_count,
    qkv_state,
    qv_bias_state,
    out_state,
    up_state,
    up_bias_state,
    down_state,
    vector_state,
):
    bf = jnp.bfloat16
    fl = jnp.float32
    w_qkv, b_qv, w_out, w_up, b_up, w_down, vectors = (
        lax.all_gather(qkv_state[0].astype(bf), "dp", axis=0, tiled=True),
        lax.all_gather(qv_bias_state[0].astype(bf), "dp", axis=2, tiled=True),
        lax.all_gather(out_state[0].astype(bf), "dp", axis=1, tiled=True),
        lax.all_gather(up_state[0].astype(bf), "dp", axis=0, tiled=True),
        lax.all_gather(up_bias_state[0].astype(bf), "dp", axis=1, tiled=True),
        lax.all_gather(down_state[0].astype(bf), "dp", axis=1, tiled=True),
        lax.all_gather(vector_state[0].astype(bf), "dp", axis=1, tiled=True),
    )
    count, length, width_model = hidden_in.shape
    rows = count * length
    heads_local = b_qv.shape[1]
    head_width = heads_local * HD
    ff_local = w_up.shape[1]
    scale = HD ** (-0.5)
    plain = hidden_in.reshape(rows, width_model)
    cotangent = out_grad.reshape(rows, width_model)
    vec = vectors.astype(fl)
    proj = jnp.einsum("td,dcf->tcf", plain, w_qkv, preferred_element_type=fl)
    bias_f = b_qv.astype(fl).reshape(2, head_width)
    bias = jnp.stack([bias_f[0], jnp.zeros((head_width,), fl), bias_f[1]])
    proj_b = (proj + bias[None]).astype(bf)
    heads = proj_b.reshape(count, length, 3, heads_local, HD)
    query = heads[:, :, 0]
    key_rows = heads[:, :, 1]
    value_rows = heads[:, :, 2]
    scores = scores_of(query, key_rows, segment_ids)
    top = jnp.max(scores, axis=-1, keepdims=True)
    expd = jnp.exp(scores - top)
    denom = jnp.sum(expd, axis=-1, keepdims=True)
    log_total = top + jnp.log(denom)
    probs_b = (expd / denom).astype(bf)
    context = (
        jnp.einsum("bhqk,bkhd->bqhd", probs_b, value_rows, preferred_element_type=fl)
        .astype(bf)
        .reshape(rows, head_width)
    )
    attn_part = jnp.dot(context, w_out, preferred_element_type=fl)
    attn = lax.psum(attn_part.astype(jnp.bfloat16), "tensor").astype(jnp.float32)
    first, first_pull = jax.vjp(layer_norm, plain.astype(fl) + attn + vec[4], vec[0], vec[1])
    first_b = first.astype(bf)
    up = jnp.dot(first_b, w_up, preferred_element_type=fl) + b_up.astype(fl).reshape(ff_local)
    act, gelu_pull = jax.vjp(gelu_exact, up)
    act_b = act.astype(bf)
    ffn_part = jnp.dot(act_b, w_down, preferred_element_type=fl)
    ffn = lax.psum(ffn_part.astype(jnp.bfloat16), "tensor").astype(jnp.float32)
    out, second_pull = jax.vjp(layer_norm, first + ffn + vec[5], vec[2], vec[3])
    grad_r2, grad_g2, grad_b2 = second_pull(cotangent.astype(fl))
    grad_ffn = grad_r2.astype(bf)
    grad_down = contract_rows(act_b, grad_ffn)
    grad_act = contract_cols(grad_ffn, w_down)
    grad_up_b = gelu_pull(grad_act)[0].astype(bf)
    grad_wup = contract_rows(first_b, grad_up_b)
    grad_bup = jnp.sum(grad_up_b, axis=0, dtype=fl).reshape(b_up.shape)
    feed_part = contract_cols(grad_up_b, w_up)
    feed_back = lax.psum(feed_part.astype(jnp.bfloat16), "tensor").astype(jnp.float32)
    grad_first = grad_r2 + feed_back.astype(bf).astype(fl)
    grad_r1, grad_g1, grad_b1 = first_pull(grad_first)
    grad_attn = grad_r1.astype(bf)
    grad_wout = contract_rows(context, grad_attn)
    grad_context = (
        contract_cols(grad_attn, w_out).astype(bf).reshape(count, length, heads_local, HD)
    )
    again = scores_of(query, key_rows, segment_ids)
    probs = jnp.exp(again - log_total)
    probs_again = probs.astype(bf)
    grad_probs = jnp.einsum("bqhd,bkhd->bhqk", grad_context, value_rows, preferred_element_type=fl)
    grad_value = jnp.einsum("bhqk,bqhd->bkhd", probs_again, grad_context, preferred_element_type=fl)
    row_dot = jnp.sum(probs * grad_probs, axis=-1, keepdims=True)
    grad_scores = (probs * (grad_probs - row_dot)).astype(bf)
    grad_query = (
        jnp.einsum("bhqk,bkhd->bqhd", grad_scores, key_rows, preferred_element_type=fl) * scale
    )
    grad_key = jnp.einsum("bhqk,bqhd->bkhd", grad_scores, query, preferred_element_type=fl) * scale
    grad_proj = (
        jnp.stack([grad_query, grad_key, grad_value], axis=2)
        .astype(bf)
        .reshape(rows, 3, head_width)
    )
    proj_sums = jnp.sum(grad_proj, axis=0, dtype=fl)
    grad_bqv = jnp.stack([proj_sums[0], proj_sums[2]]).reshape(2, heads_local, HD)
    grad_wqkv = jnp.einsum("td,tcf->dcf", plain, grad_proj, preferred_element_type=fl)
    input_part = jnp.einsum("tcf,dcf->td", grad_proj, w_qkv, preferred_element_type=fl)
    vec_part = jnp.stack(
        [grad_g1, grad_b1, grad_g2, grad_b2, jnp.sum(grad_r1, axis=0), jnp.sum(grad_r2, axis=0)]
    )
    input_back = lax.psum(input_part.astype(jnp.bfloat16), "tensor").astype(jnp.float32)
    grad_in = (grad_r1 + input_back.astype(bf).astype(fl)).astype(bf).reshape(hidden_in.shape)
    hidden_out = out.astype(bf).reshape(hidden_in.shape)
    summed = (
        lax.psum_scatter(grad_wqkv, "dp", scatter_dimension=0, tiled=True),
        lax.psum_scatter(grad_bqv, "dp", scatter_dimension=2, tiled=True),
        lax.psum_scatter(grad_wout, "dp", scatter_dimension=1, tiled=True),
        lax.psum_scatter(grad_wup, "dp", scatter_dimension=0, tiled=True),
        lax.psum_scatter(grad_bup, "dp", scatter_dimension=1, tiled=True),
        lax.psum_scatter(grad_down, "dp", scatter_dimension=1, tiled=True),
        lax.psum_scatter(vec_part, "dp", scatter_dimension=1, tiled=True),
    )
    steps_f = step_count[0].astype(fl)
    factor = jnp.minimum(steps_f / warm_steps, (total_steps - steps_f) / (total_steps - warm_steps))
    fix_first = 1.0 - jnp.exp(steps_f * math.log(beta_first))
    fix_second = 1.0 - jnp.exp(steps_f * math.log(beta_second))
    states = (
        qkv_state,
        qv_bias_state,
        out_state,
        up_state,
        up_bias_state,
        down_state,
        vector_state,
    )
    news = tuple((moment_update(s, g) for s, g in zip(states, summed)))
    plan = jnp.stack([factor, fix_first, fix_second])
    return (
        hidden_out,
        grad_in,
        summed[0],
        summed[1],
        summed[2],
        summed[3],
        summed[4],
        summed[5],
        summed[6],
        news[0],
        news[1],
        news[2],
        news[3],
        news[4],
        news[5],
        news[6],
        plan,
    )


def solution(mesh):
    return jax.shard_map(
        body,
        mesh=mesh,
        in_specs=(
            P("dp", None, None),
            P("dp", None, None),
            P("dp", None),
            P(),
            P(None, "dp", None, "tensor"),
            P(None, None, "tensor", "dp"),
            P(None, "tensor", "dp"),
            P(None, "dp", "tensor"),
            P(None, "tensor", "dp"),
            P(None, "tensor", "dp"),
            P(None, None, "dp"),
        ),
        out_specs=(
            P("dp", None, None),
            P("dp", None, None),
            P("dp", None, "tensor"),
            P(None, "tensor", "dp"),
            P("tensor", "dp"),
            P("dp", "tensor"),
            P("tensor", "dp"),
            P("tensor", "dp"),
            P(None, "dp"),
            P(None, "dp", None, "tensor"),
            P(None, None, "tensor", "dp"),
            P(None, "tensor", "dp"),
            P(None, "dp", "tensor"),
            P(None, "tensor", "dp"),
            P(None, "tensor", "dp"),
            P(None, None, "dp"),
            P(),
        ),
        check_vma=False,
    )
```

profile of v0, /device:TPU:0, one launch (start us, length us, event | category | flops | bytes accessed | tf_op | source)
XLA Modules:
  0.0 760.8 jit_solution(6386560561636301362)
XLA Ops:
  9.0 10.6 %all-gather.1 = bf16[1,2,3,64]{2,1,0,3:T(2,128)(2,1)S(1)} all-gather(bf16[1,2,3,8]{2,1,0,3:T(2,128)(2,1)S(1)} %copy.181), channel_id=3, replica_groups=mesh['dp'=8,'tensor'=4] {'dp'}, dimensions={3}, use_global_device_ids=true | all-gather | bytes 864 | tf_op jit(solution)/shard_map/all_gather | solution.py:68
  22.8 11.3 %all-gather.2 = bf16[1,192,768]{1,0,2:T(2,128)(2,1)} all-gather(bf16[1,192,96]{1,0,2:T(2,128)(2,1)S(1)} %copy.142), channel_id=4, replica_groups=mesh['dp'=8,'tensor'=4] {'dp'}, dimensions={2}, use_global_device_ids=true | all-gather | bytes 331776 | tf_op jit(solution)/shard_map/all_gather | solution.py:69
  34.1 2.2 copy.143
  36.3 2.3 broadcast_compare_fusion
  38.6 15.8 %all-gather = bf16[1,768,3,192]{3,2,0,1:T(4,128)(2,1)} all-gather(bf16[1,96,3,192]{3,2,0,1:T(4,128)(2,1)} %copy.132), channel_id=2, replica_groups=mesh['dp'=8,'tensor'=4] {'dp'}, dimensions={1}, use_global_device_ids=true | all-gather | bytes 995328 | tf_op jit(solution)/shard_map/all_gather | solution.py:67
  54.4 3.4 copy.133
  57.9 3.2 fusion.74
  61.2 1.7 add_convert_fusion.5
  62.9 6.2 reshape.215
  69.1 2.4 fusion.69
  71.5 4.4 fusion.73
  76.0 1.8 fusion
  77.8 2.8 copy-done
  80.7 2.3 fusion.22
  84.7 2.7 convolution_convert_fusion.2
  87.5 1.6 slice.205
  89.3 1.6 slice.204
  93.2 8.7 %all-gather.5 = bf16[1,6,128]{1,0,2:T(2,128)(2,1)S(1)} all-gather(bf16[1,6,16]{1,0,2:T(2,128)(2,1)} %copy.145), channel_id=7, replica_groups=mesh['dp'=8,'tensor'=4] {'dp'}, dimensions={2}, use_global_device_ids=true | all-gather | bytes 1728 | tf_op jit(solution)/shard_map/all_gather | solution.py:71
  103.2 10.8 %all-gather.3 = bf16[1,6,768]{1,0,2:T(2,128)(2,1)S(1)} all-gather(bf16[1,6,96]{1,0,2:T(2,128)(2,1)S(1)} %copy.185), channel_id=5, replica_groups=mesh['dp'=8,'tensor'=4] {'dp'}, dimensions={2}, use_global_device_ids=true | all-gather | bytes 10368 | tf_op jit(solution)/shard_map/all_gather | solution.py:73
  114.4 13.0 %slice_reduce_fusion.1 = (f32[768]{0:T(1024)S(1)}, f32[768]{0:T(1024)S(1)}, f32[768]{0:T(1024)S(1)}, f32[768]{0:T(1024)S(1)}, f32[768]{0:T(1024)S(1)}, /*index=5*/f32[768]{0:T(1024)S(1)}) fusion(f32[1,6,768]{1,0,2:T(1,128)S(1)} %convert_element_type.169), kind=kLoop, calls=%fused_computation.78 | loop fusion | bytes 36864 | tf_op jit(solution)/shard_map/slice | solution.py:112
  127.4 81.6 %all-reduce.6.cloned.1.call-done = bf16[2048,768]{1,0:T(8,128)(2,1)} async-done(((bf16[2048,768]{1,0:T(8,128)(2,1)}), bf16[2048,768]{1,0:T(8,128)(2,1)}) %all-reduce.6.cloned.1.call-update) | async-done | bytes 3145744 | tf_op jit(solution)/shard_map/psum | solution.py:104
  209.0 3.1 fusion.11
  212.1 3.7 multiply_reduce_fusion.4
  215.8 7.4 multiply_convert_fusion.1
  223.3 6.2 convolution_convert_fusion.1
  229.7 120.0 %all-reduce.8.cloned.1.call-done = bf16[2048,768]{1,0:T(8,128)(2,1)} async-done(((bf16[2048,768]{1,0:T(8,128)(2,1)}), bf16[2048,768]{1,0:T(8,128)(2,1)}) %all-reduce.8.cloned.1.call-update) | async-done | bytes 3145744 | tf_op jit(solution)/shard_map/psum | solution.py:111
  349.7 4.8 fusion.67
  356.4 3.0 fusion.7
  359.5 4.3 fusion.66
  363.8 5.9 convert_reduce_fusion.1
  369.7 1.7 copy-done.35
  371.5 4.0 convolution_convert_fusion
  376.4 8.0 %fusion.60 = f32[768,768]{0,1:T(8,128)} fusion(bf16[2048,768]{1,0:T(8,128)(2,1)} %copy-done.36, f32[2048,768]{1,0:T(8,128)} %copy-done.2, f32[2048]{0:T(1024)S(1)} %negate_multiply_fusion.1), kind=kOutput, calls=%fused_computation.147 | convolution fusion | flops 2419064832 | bytes 11804672 | tf_op jit(solution)/shard_map/dot_general | solution.py:34
  384.5 8.0 %fusion.61 = f32[768,768]{1,0:T(8,128)} fusion(bf16[2048,768]{1,0:T(8,128)(2,1)} %copy-done.35, f32[2048,768]{1,0:T(8,128)} %get-tuple-element.123, f32[768]{0:T(1024)} %copy-done.24, f32[768]{0:T(1024)} %copy-done.22, f32[2048]{0:T(1024)S(1)} %fusion.49), kind=kOutput, calls=%fused_computation.148 | convolution fusion | flops 2422210560 | bytes 11810816 | tf_op jit(solution)/shard_map/dot_general | solution.py:34
  392.8 102.9 %all-reduce.10.cloned.1.call-done = bf16[2048,768]{1,0:T(8,128)(2,1)} async-done(((bf16[2048,768]{1,0:T(8,128)(2,1)}), bf16[2048,768]{1,0:T(8,128)(2,1)}) %all-reduce.10.cloned.1.call-update) | async-done | bytes 3145744 | tf_op jit(solution)/shard_map/psum | solution.py:121
  495.7 8.0 %multiply_reduce_fusion.1 = (f32[768]{0:T(1024)}, f32[2048]{0:T(1024)S(1)}, f32[768]{0:T(1024)}, f32[768]{0:T(1024)}) fusion(f32[2048,768]{1,0:T(8,128)} %get-tuple-element.123, f32[2048]{0:T(1024)S(1)} %fusion.49, bf16[2048,768]{1,0:T(8,128)(2,1)} %all-reduce.10.cloned.1.call-done, f32[2048,768]{1,0:T(8,128)} %copy-done.2, ...), kind=kLoop, calls=%fused_computation.19 | loop fusion | flops 17297152 | bytes 15765504 | tf_op jit(solution)/shard_map/transpose(jvp())/reduce_sum | solution.py:18
  503.7 6.1 fusion.65
  509.8 2.6 copy-done.3
  512.4 2.2 convolution_convert_fusion.3
  514.7 3.0 reshape.218
  517.6 8.3 %multiply_reduce_fusion = (f32[4,3,512]{2,1,0:T(4,128)S(1)}, f32[4,3,512,512]{2,3,1,0:T(8,128)S(1)}) fusion(f32[4,3,512,512]{2,3,1,0:T(8,128)} %copy-done, f32[4,3,512]{2,1,0:T(4,128)S(1)} %log_add_fusion, bf16[4,512,1,3,64]{1,0,4,3,2:T(4,128)(2,1)} %copy-done.11, bf16[4,512,3,64]{1,0,3,2:T(4,128)(2,1)} %reshape.218), kind=kOutput, calls=%fused_computation.1 | convolution fusion | flops 412084224 | bytes 26787840 | tf_op jit(solution)/shard_map/bqhd,bkhd->bhqk/dot_general | solution.py:132
  526.0 6.9 multiply_convert_fusion
  532.9 2.6 copy-done.1
  536.6 1.5 copy.149
  538.1 3.2 stack.101
  541.3 5.1 fusion.21
  546.3 1.5 copy.151
  547.8 2.8 stack.102
  550.6 2.1 constant_dynamic-update-slice_fusion.2
  552.8 5.6 convolution_bitcast_fusion
  558.4 7.7 %fusion.17 = bf16[4,512,3,64]{1,3,2,0:T(8,128)(2,1)} fusion(f32[4,3,512,512]{2,3,1,0:T(8,128)} %copy-done, f32[4,3,512]{2,1,0:T(4,128)S(1)} %log_add_fusion, bf16[4,512,3,64]{1,0,3,2:T(4,128)(2,1)} %reshape.218), kind=kOutput, calls=%fused_computation.53 | convolution fusion | flops 409337856 | bytes 14180352 | tf_op jit(solution)/shard_map/bhqk,bqhd->bkhd/dot_general | solution.py:133
  566.2 2.1 constant_dynamic-update-slice_fusion.1
  568.3 2.6 copy.154
  570.9 2.8 stack.103
  573.7 2.1 constant_dynamic-update-slice_fusion
  575.8 5.8 fusion.75
  581.7 2.8 copy.179
  585.8 6.2 bitcast_convert_fusion
  595.1 1.2 dynamic-slice
  601.6 14.3 %all-reduce = f32[2,3,64]{2,1,0:T(4,128)S(1)} all-reduce(f32[2,3,64]{2,1,0:T(4,128)S(1)} %reshape.220), channel_id=10, replica_groups=mesh['dp'=8,'tensor'=4] {'dp'}, use_global_device_ids=true, to_apply=%region_17.18.clone | all-reduce | flops 384 | bytes 3072
  623.8 19.7 %reduce-scatter.20.cloned.1.call-done = f32[96,576]{1,0:T(8,128)} async-done(((f32[768,576]{1,0:T(8,128)}), f32[96,576]{1,0:T(8,128)}) %reduce-scatter.20.cloned.1.call-update) | async-done | bytes 221200
  644.8 67.8 %all-reduce.12.cloned.1.call-done = bf16[2048,768]{1,0:T(8,128)(2,1)} async-done(((bf16[2048,768]{1,0:T(8,128)(2,1)}), bf16[2048,768]{1,0:T(8,128)(2,1)}) %all-reduce.12.cloned.1.call-update) | async-done | bytes 3145744 | tf_op jit(solution)/shard_map/psum | solution.py:152
  712.5 5.4 add_reduce_fusion
  721.0 31.0 %reduce-scatter.26.cloned.1.call-done = f32[96,6]{1,0:T(8,128)} async-done(((f32[768,6]{1,0:T(8,128)}), f32[96,6]{1,0:T(8,128)}) %reduce-scatter.26.cloned.1.call-update) | async-done | bytes 2320
  (180 shorter events, 36.6 us)
Async XLA Ops:
  8.0 49.9 %copy-start.6 = (bf16[4,512,768]{2,1,0:T(8,128)(2,1)S(1)}, bf16[4,512,768]{2,1,0:T(8,128)(2,1)}, u32[]{:S(2)}) copy-start(bf16[4,512,768]{2,1,0:T(8,128)(2,1)} %param.11) | copy-start | bytes 9437188
  8.0 200.9 %all-reduce.6.cloned.1.call-start = ((), (), s32[]{:S(2)}) async-start(), calls=%async_computation.6 | async-start | bytes 6291456 | tf_op jit(solution)/shard_map/psum | solution.py:104
  71.5 4.4 copy-start.9
  71.5 4.4 copy-start.12
  71.5 6.3 copy-start.11
  76.0 4.7 copy-start
  76.0 4.7 copy-start.16
  77.8 5.3 copy-start.18
  83.9 0.9 copy-start.8
  87.5 128.3 %all-gather.10.cloned.1.call-start = ((), (), s32[]{:S(2)}) async-start(), calls=%async_computation.12 | async-start | bytes 1327104 | tf_op jit(solution)/shard_map/all_gather | solution.py:70
  89.2 134.1 %all-gather.12.cloned.1.call-start = ((), (), s32[]{:S(2)}) async-start(), calls=%async_computation.13 | async-start | bytes 1327104 | tf_op jit(solution)/shard_map/all_gather | solution.py:72
  90.9 258.8 %all-reduce.8.cloned.1.call-start = ((), (), s32[]{:S(2)}) async-start(), calls=%async_computation.7 | async-start | bytes 6291456 | tf_op jit(solution)/shard_map/psum | solution.py:111
  127.3 222.4 %copy-start.22 = (f32[768]{0:T(1024)}, f32[768]{0:T(1024)S(1)}, u32[]{:S(2)}) copy-start(f32[768]{0:T(1024)S(1)} %get-tuple-element.111) | copy-start | bytes 9220
  127.3 222.4 %copy-start.24 = (f32[768]{0:T(1024)}, f32[768]{0:T(1024)S(1)}, u32[]{:S(2)}) copy-start(f32[768]{0:T(1024)S(1)} %get-tuple-element.110) | copy-start | bytes 9220
  208.9 3.2 copy-start.7
  215.8 7.5 copy-start.20
  223.3 6.2 copy-start.36
  229.5 266.2 %all-reduce.10.cloned.1.call-start = ((), (), s32[]{:S(2)}) async-start(), calls=%async_computation.8 | async-start | bytes 6291456 | tf_op jit(solution)/shard_map/psum | solution.py:121
  354.5 1.9 copy-start.4
  356.4 7.4 slice-start
  359.4 4.3 copy-start.34
  359.4 4.3 slice-start.1
  363.8 6.0 copy-start.2
  363.8 7.7 %copy-start.33 = (bf16[1,768,768]{2,1,0:T(8,128)(2,1)S(1)}, bf16[1,768,768]{2,1,0:T(8,128)(2,1)}, u32[]{:S(2)}) copy-start(bf16[1,768,768]{2,1,0:T(8,128)(2,1)} %all-gather.10.cloned.1.call-done) | copy-start | bytes 3538948
  369.7 1.8 copy-start.35
  375.5 222.1 %reduce-scatter.24.cloned.1.call-start = ((), (), s32[]{:S(2)}) async-start(), calls=%async_computation.16 | async-start | bytes 73728
  376.3 8.1 %copy-start.17 = (f32[4,3,512]{2,1,0:T(4,128)S(1)}, f32[4,3,512]{2,1,0:T(4,128)}, u32[]{:S(2)}) copy-start(f32[4,3,512]{2,1,0:T(4,128)} %copy-done.16) | copy-start | bytes 73732
  376.4 8.1 %copy-start.19 = (f32[4,3,512]{2,1,0:T(4,128)S(1)}, f32[4,3,512]{2,1,0:T(4,128)}, u32[]{:S(2)}) copy-start(f32[4,3,512]{2,1,0:T(4,128)} %copy-done.18) | copy-start | bytes 73732
  376.4 241.5 %reduce-scatter.18.cloned.1.call-start = ((), (), s32[]{:S(2)}) async-start(), calls=%async_computation.11 | async-start | bytes 2654208 | tf_op jit(solution)/shard_map/reduce_scatter | solution.py:161
  384.4 235.6 %reduce-scatter.16.cloned.1.call-start = ((), (), s32[]{:S(2)}) async-start(), calls=%async_computation.10 | async-start | bytes 2654208 | tf_op jit(solution)/shard_map/reduce_scatter | solution.py:159
  384.5 111.2 %copy-start.23 = (f32[768]{0:T(1024)S(1)}, f32[768]{0:T(1024)}, u32[]{:S(2)}) copy-start(f32[768]{0:T(1024)} %copy-done.22) | copy-start | bytes 9220
  392.5 111.2 %copy-start.21 = (f32[2048]{0:T(1024)S(1)}, f32[2048]{0:T(1024)}, u32[]{:S(2)}) copy-start(f32[2048]{0:T(1024)} %copy-done.20) | copy-start | bytes 24580
  392.6 229.5 %reduce-scatter.22.cloned.1.call-start = ((), (), s32[]{:S(2)}) async-start(), calls=%async_computation.15 | async-start | bytes 884736
  495.7 8.0 %copy-start.5 = (bf16[2048,768]{1,0:T(8,128)(2,1)S(1)}, bf16[2048,768]{1,0:T(8,128)(2,1)}, u32[]{:S(2)}) copy-start(bf16[2048,768]{1,0:T(8,128)(2,1)} %all-reduce.10.cloned.1.call-done) | copy-start | bytes 9437188
  509.8 2.6 copy-start.3
  526.0 9.5 %copy-start.13 = (bf16[4,512,1,3,64]{1,0,4,3,2:T(4,128)(2,1)S(1)}, bf16[4,512,1,3,64]{1,0,4,3,2:T(4,128)(2,1)}, u32[]{:S(2)}) copy-start(bf16[4,512,1,3,64]{1,0,4,3,2:T(4,128)(2,1)} %copy-done.12) | copy-start | bytes 2359300
  532.9 2.6 copy-start.1
  566.2 77.4 %reduce-scatter.20.cloned.1.call-start = ((), (), s32[]{:S(2)}) async-start(), calls=%async_computation.14 | async-start | bytes 2211840
  584.5 128.0 %all-reduce.12.cloned.1.call-start = ((), (), s32[]{:S(2)}) async-start(), calls=%async_computation.9 | async-start | bytes 6291456 | tf_op jit(solution)/shard_map/psum | solution.py:152
  585.8 8.3 %copy-start.27 = (f32[768]{0:T(1024)S(1)}, f32[768]{0:T(1024)}, u32[]{:S(2)}) copy-start(f32[768]{0:T(1024)} %convert_reduce_fusion) | copy-start | bytes 9220
  585.8 11.7 %copy-start.25 = (f32[768]{0:T(1024)S(1)}, f32[768]{0:T(1024)}, u32[]{:S(2)}) copy-start(f32[768]{0:T(1024)} %get-tuple-element.104) | copy-start | bytes 9220
  585.8 15.2 %copy-start.26 = (f32[768]{0:T(1024)S(1)}, f32[768]{0:T(1024)}, u32[]{:S(2)}) copy-start(f32[768]{0:T(1024)} %get-tuple-element.107) | copy-start | bytes 9220
  592.1 9.0 %copy-start.10 = (bf16[2048,3,192]{0,2,1:T(8,128)(2,1)S(1)}, bf16[2048,3,192]{0,2,1:T(8,128)(2,1)}, u32[]{:S(2)}) copy-start(bf16[2048,3,192]{0,2,1:T(8,128)(2,1)} %constant_dynamic-update-slice_fusion) | copy-start | bytes 7077892
  592.1 31.0 %copy-start.15 = (f32[3,192,96]{2,1,0:T(8,128)S(1)}, f32[3,192,96]{2,1,0:T(8,128)}, u32[]{:S(2)}) copy-start(f32[3,192,96]{2,1,0:T(8,128)} %param.17) | copy-start | bytes 663556
  592.1 159.8 %reduce-scatter.26.cloned.1.call-start = ((), (), s32[]{:S(2)}) async-start(), calls=%async_computation.17 | async-start | bytes 442368
  598.4 119.6 %copy-start.28 = (f32[6,16]{1,0:T(8,128)}, f32[6,16]{1,0:T(8,128)S(1)}, u32[]{:S(2)}) copy-start(f32[6,16]{1,0:T(8,128)S(1)} %copy.176) | copy-start | bytes 1156
  616.6 101.3 %copy-start.30 = (f32[2,3,8]{2,0,1:T(2,128)}, f32[2,3,8]{2,0,1:T(2,128)S(1)}, u32[]{:S(2)}) copy-start(f32[2,3,8]{2,0,1:T(2,128)S(1)} %get-tuple-element.115) | copy-start | bytes 580
  623.1 94.8 %copy-start.14 = (f32[192,96]{1,0:T(8,128)}, f32[192,96]{1,0:T(8,128)S(1)}, u32[]{:S(2)}) copy-start(f32[192,96]{1,0:T(8,128)S(1)} %copy.174) | copy-start | bytes 221188
  644.7 73.2 %copy-start.31 = (f32[1,768]{1,0:T(1,128)S(1)}, f32[1,768]{1,0:T(1,128)}, u32[]{:S(2)}) copy-start(f32[1,768]{1,0:T(1,128)} %reshape.225) | copy-start | bytes 9220
  644.7 108.1 %copy-start.32 = (f32[3,6,96]{2,1,0:T(8,128)S(1)}, f32[3,6,96]{2,1,0:T(8,128)}, u32[]{:S(2)}) copy-start(f32[3,6,96]{2,1,0:T(8,128)} %param.21) | copy-start | bytes 20740
  752.8 0.6 copy-start.29
Sparse Core Ops, SparseCore 0:
  87.6 121.2 all-reduce.5
  229.6 120.0 all-reduce.7
  375.6 120.0 all-reduce.9
  592.2 120.2 all-reduce.11
Sparse Core Ops, SparseCore 1:
  90.4 25.2 all-gather.9
  118.0 23.8 all-gather.11
  379.6 32.5 reduce-scatter.23
  416.1 42.2 reduce-scatter.17
  462.2 42.2 reduce-scatter.15
  566.2 33.9 reduce-scatter.21
  603.5 40.0 reduce-scatter.19
  719.0 32.9 reduce-scatter.25
where the time goes:
time: 772 us; the launch traced here: 761 us
  waiting for transfers between devices  423 us (55%)
  matrix products  94.3 us (12%)
  local copies, waits for them, and re-layouts  90.2 us (12%)
  blocking collectives  71.4 us (9%)
  other arithmetic  63 us (8%)
  between operations  17.6 us (2%)
    psum x1, waiting for transfers between devices, body(): ffn = lax.psum(ffn_part.astype(jnp.bfloat16), 'tensor').astype(jnp.float32)  120 us
    psum x1, waiting for transfers between devices, body(): lax.psum(feed_part.astype(jnp.bfloat16), 'tensor').astype(jnp.float32)  103 us
    psum x1, waiting for transfers between devices, body(): lax.psum(attn_part.astype(jnp.bfloat16), 'tensor').astype(jnp.float32)  81.6 us
    psum x1, waiting for transfers between devices, body(): lax.psum(input_part.astype(jnp.bfloat16), 'tensor').astype(jnp.float32)  67.8 us
    unnamed x16, waiting for transfers between devices  50.9 us
    unnamed x98, local copies, waits for them, and re-layouts  29.5 us
    reduce_sum x4, other arithmetic, layer_norm(): center = value - jnp.mean(value, axis=-1, keepdims=True)  18.3 us
    dot_general x2, matrix products, contract_rows(): lax.dot_general(left, right, (((0,), (0,)), ((), ())), preferred_element_...  16 us
  transfers between devices with their start and end apart: 12, of which 6 were waited for; matrix products, arithmetic and copies ran while one was open for 21% of the time, Pallas kernels for 0%

commit v1 on v0

--- a/solution.py
+++ b/solution.py
@@ -10,6 +10,12 @@
 beta_second = 0.999
 warm_steps = 10000.0
 total_steps = 200000.0
+
+
+def _remake_pairs_all(my_data):
+    vec_out = jax.lax.all_gather(my_data, axis_name="tensor")
+    x_new = jnp.sum(vec_out, axis=0)
+    return x_new
 
 
 def layer_norm(value, gain, shift):
@@ -108,7 +114,7 @@
     act, gelu_pull = jax.vjp(gelu_exact, up)
     act_b = act.astype(bf)
     ffn_part = jnp.dot(act_b, w_down, preferred_element_type=fl)
-    ffn = lax.psum(ffn_part.astype(jnp.bfloat16), "tensor").astype(jnp.float32)
+    ffn = _remake_pairs_all(ffn_part.astype(jnp.bfloat16)).astype(jnp.float32)
     out, second_pull = jax.vjp(layer_norm, first + ffn + vec[5], vec[2], vec[3])
     grad_r2, grad_g2, grad_b2 = second_pull(cotangent.astype(fl))
     grad_ffn = grad_r2.astype(bf)

time: 772 us -> 877 us (1.14)
  waiting for transfers between devices: 423 us -> 519 us
    all_gather x0 -> x1, waiting for transfers between devices: none -> 217 us  [_remake_pairs_all(): vec_out = jax.lax.all_gather(my_data, axis_name='tensor')]
    psum x1 -> x0, waiting for transfers between devices: 120 us -> none  [body(): ffn = lax.psum(ffn_part.astype(jnp.bfloat16), 'tensor').astype(jnp.float32)]
  transfers between devices with their start and end apart: 12 -> 12, of which waited for: 6 -> 6; matrix products, arithmetic and copies ran while one was open for 21% -> 19% of each run, Pallas kernels for 0% -> 0%
where the time goes in v1:
time: 877 us; the launch traced here: 865 us
  waiting for transfers between devices  519 us (59%)
  matrix products  94.8 us (11%)
  local copies, waits for them, and re-layouts  90 us (10%)
  blocking collectives  70.9 us (8%)
  other arithmetic  70.8 us (8%)
  between operations  17.9 us (2%)
    all_gather x1, waiting for transfers between devices, _remake_pairs_all(): vec_out = jax.lax.all_gather(my_data, axis_name='tensor')  217 us
    psum x1, waiting for transfers between devices, body(): lax.psum(feed_part.astype(jnp.bfloat16), 'tensor').astype(jnp.float32)  102 us
    psum x1, waiting for transfers between devices, body(): lax.psum(attn_part.astype(jnp.bfloat16), 'tensor').astype(jnp.float32)  82 us
    psum x1, waiting for transfers between devices, body(): lax.psum(input_part.astype(jnp.bfloat16), 'tensor').astype(jnp.float32)  67.9 us
    unnamed x16, waiting for transfers between devices  50.8 us
    unnamed x98, local copies, waits for them, and re-layouts  29.4 us
  transfers between devices with their start and end apart: 12, of which 6 were waited for; matrix products, arithmetic and copies ran while one was open for 19% of the time, Pallas kernels for 0%

profile of v1, /device:TPU:0, one launch (start us, length us, event | category | flops | bytes accessed | tf_op | source)
XLA Modules:
  0.0 864.9 jit_solution(9425358926136026017)
XLA Ops:
  9.0 10.6 %all-gather.1 = bf16[1,2,3,64]{2,1,0,3:T(2,128)(2,1)S(1)} all-gather(bf16[1,2,3,8]{2,1,0,3:T(2,128)(2,1)S(1)} %copy.181), channel_id=3, replica_groups=mesh['dp'=8,'tensor'=4] {'dp'}, dimensions={3}, use_global_device_ids=true | all-gather | bytes 864 | tf_op jit(solution)/shard_map/all_gather | solution.py:74
  22.8 11.3 %all-gather.2 = bf16[1,192,768]{1,0,2:T(2,128)(2,1)} all-gather(bf16[1,192,96]{1,0,2:T(2,128)(2,1)S(1)} %copy.142), channel_id=4, replica_groups=mesh['dp'=8,'tensor'=4] {'dp'}, dimensions={2}, use_global_device_ids=true | all-gather | bytes 331776 | tf_op jit(solution)/shard_map/all_gather | solution.py:75
  34.1 2.2 copy.143
  36.3 2.3 broadcast_compare_fusion
  38.6 15.8 %all-gather = bf16[1,768,3,192]{3,2,0,1:T(4,128)(2,1)} all-gather(bf16[1,96,3,192]{3,2,0,1:T(4,128)(2,1)} %copy.132), channel_id=2, replica_groups=mesh['dp'=8,'tensor'=4] {'dp'}, dimensions={1}, use_global_device_ids=true | all-gather | bytes 995328 | tf_op jit(solution)/shard_map/all_gather | solution.py:73
  54.4 3.4 copy.133
  57.9 3.2 fusion.74
  61.1 1.7 add_convert_fusion.5
  62.9 6.2 reshape.215
  69.0 2.4 fusion.69
  71.5 4.4 fusion.73
  75.9 1.8 fusion
  77.8 2.8 copy-done
  80.7 2.3 fusion.22
  84.7 2.7 convolution_convert_fusion.2
  87.5 1.6 slice.205
  89.2 1.6 slice.204
  93.1 8.7 %all-gather.5 = bf16[1,6,128]{1,0,2:T(2,128)(2,1)S(1)} all-gather(bf16[1,6,16]{1,0,2:T(2,128)(2,1)} %copy.145), channel_id=7, replica_groups=mesh['dp'=8,'tensor'=4] {'dp'}, dimensions={2}, use_global_device_ids=true | all-gather | bytes 1728 | tf_op jit(solution)/shard_map/all_gather | solution.py:77
  103.2 10.3 %all-gather.3 = bf16[1,6,768]{1,0,2:T(2,128)(2,1)S(1)} all-gather(bf16[1,6,96]{1,0,2:T(2,128)(2,1)S(1)} %copy.185), channel_id=5, replica_groups=mesh['dp'=8,'tensor'=4] {'dp'}, dimensions={2}, use_global_device_ids=true | all-gather | bytes 10368 | tf_op jit(solution)/shard_map/all_gather | solution.py:79
  113.9 13.0 %slice_reduce_fusion.1 = (f32[768]{0:T(1024)S(1)}, f32[768]{0:T(1024)S(1)}, f32[768]{0:T(1024)S(1)}, f32[768]{0:T(1024)S(1)}, f32[768]{0:T(1024)S(1)}, /*index=5*/f32[768]{0:T(1024)S(1)}) fusion(f32[1,6,768]{1,0,2:T(1,128)S(1)} %convert_element_type.171), kind=kLoop, calls=%fused_computation.78 | loop fusion | bytes 36864 | tf_op jit(solution)/shard_map/slice | solution.py:118
  126.9 82.0 %all-reduce.5.cloned.1.call-done = bf16[2048,768]{1,0:T(8,128)(2,1)} async-done(((bf16[2048,768]{1,0:T(8,128)(2,1)}), bf16[2048,768]{1,0:T(8,128)(2,1)}) %all-reduce.5.cloned.1.call-update) | async-done | bytes 3145744 | tf_op jit(solution)/shard_map/psum | solution.py:110
  208.9 3.1 fusion.11
  212.1 3.8 multiply_reduce_fusion.4
  215.9 7.4 multiply_convert_fusion.1
  223.3 6.2 convolution_convert_fusion.1
  230.0 216.9 %all-gather.16.cloned.1.call-done = bf16[8192,768]{1,0:T(8,128)(2,1)} async-done(((bf16[2048,768]{1,0:T(8,128)(2,1)}), bf16[8192,768]{1,0:T(8,128)(2,1)}) %all-gather.16.cloned.1.call-update) | async-done | bytes 12582928 | tf_op jit(solution)/shard_map/all_gather | solution.py:16
  446.9 8.6 reduce_sum.176
  455.5 3.8 fusion.67
  461.2 3.0 fusion.7
  464.3 4.3 fusion.66
  468.7 5.9 convert_reduce_fusion.1
  474.6 1.7 copy-done.35
  476.3 4.0 convolution_convert_fusion
  481.2 8.5 fusion.60
  489.8 8.0 fusion.61
  498.1 101.6 %all-reduce.7.cloned.1.call-done = bf16[2048,768]{1,0:T(8,128)(2,1)} async-done(((bf16[2048,768]{1,0:T(8,128)(2,1)}), bf16[2048,768]{1,0:T(8,128)(2,1)}) %all-reduce.7.cloned.1.call-update) | async-done | bytes 3145744 | tf_op jit(solution)/shard_map/psum | solution.py:127
  599.7 8.0 multiply_reduce_fusion.1
  607.7 6.1 fusion.65
  613.8 2.6 copy-done.3
  616.4 2.2 convolution_convert_fusion.3
  618.6 3.0 reshape.218
  621.6 8.3 multiply_reduce_fusion
  629.9 6.9 multiply_convert_fusion
  636.8 2.6 copy-done.1
  640.6 1.5 copy.149
  642.1 3.0 stack.101
  645.1 5.1 fusion.21
  650.1 1.5 copy.151
  651.6 2.8 stack.102
  654.4 2.1 constant_dynamic-update-slice_fusion.2
  656.5 5.6 convolution_bitcast_fusion
  662.2 7.8 fusion.17
  670.0 2.1 constant_dynamic-update-slice_fusion.1
  672.1 2.7 copy.154
  674.7 2.8 stack.103
  677.5 2.1 constant_dynamic-update-slice_fusion
  679.7 5.8 fusion.75
  685.5 2.8 copy.179
  689.7 6.2 bitcast_convert_fusion
  705.5 14.3 %all-reduce = f32[2,3,64]{2,1,0:T(4,128)S(1)} all-reduce(f32[2,3,64]{2,1,0:T(4,128)S(1)} %reshape.220), channel_id=11, replica_groups=mesh['dp'=8,'tensor'=4] {'dp'}, use_global_device_ids=true, to_apply=%region_17.18.clone | all-reduce | flops 384 | bytes 3072
  727.7 19.6 %reduce-scatter.20.cloned.1.call-done = f32[96,576]{1,0:T(8,128)} async-done(((f32[768,576]{1,0:T(8,128)}), f32[96,576]{1,0:T(8,128)}) %reduce-scatter.20.cloned.1.call-update) | async-done | bytes 221200
  748.6 67.9 %all-reduce.9.cloned.1.call-done = bf16[2048,768]{1,0:T(8,128)(2,1)} async-done(((bf16[2048,768]{1,0:T(8,128)(2,1)}), bf16[2048,768]{1,0:T(8,128)(2,1)}) %all-reduce.9.cloned.1.call-update) | async-done | bytes 3145744 | tf_op jit(solution)/shard_map/psum | solution.py:158
  816.4 5.4 add_reduce_fusion
  824.9 31.0 %reduce-scatter.26.cloned.1.call-done = f32[96,6]{1,0:T(8,128)} async-done(((f32[768,6]{1,0:T(8,128)}), f32[96,6]{1,0:T(8,128)}) %reduce-scatter.26.cloned.1.call-update) | async-done | bytes 2320
  (181 shorter events, 38.1 us)
Async XLA Ops:
  8.0 49.9 %copy-start.6 = (bf16[4,512,768]{2,1,0:T(8,128)(2,1)S(1)}, bf16[4,512,768]{2,1,0:T(8,128)(2,1)}, u32[]{:S(2)}) copy-start(bf16[4,512,768]{2,1,0:T(8,128)(2,1)} %param.11) | copy-start | bytes 9437188
  8.0 200.9 %all-reduce.5.cloned.1.call-start = ((), (), s32[]{:S(2)}) async-start(), calls=%async_computation.6 | async-start | bytes 6291456 | tf_op jit(solution)/shard_map/psum | solution.py:110
  71.5 4.4 copy-start.9
  71.5 4.4 copy-start.12
  71.5 6.3 copy-start.11
  75.9 4.7 copy-start
  75.9 4.7 copy-start.16
  77.7 5.3 copy-start.18
  83.8 0.9 copy-start.8
  87.5 128.4 %all-gather.12.cloned.1.call-start = ((), (), s32[]{:S(2)}) async-start(), calls=%async_computation.11 | async-start | bytes 1327104 | tf_op jit(solution)/shard_map/all_gather | solution.py:76
  89.2 134.2 %all-gather.14.cloned.1.call-start = ((), (), s32[]{:S(2)}) async-start(), calls=%async_computation.12 | async-start | bytes 1327104 | tf_op jit(solution)/shard_map/all_gather | solution.py:78
  90.9 356.0 %all-gather.16.cloned.1.call-start = ((), (), s32[]{:S(2)}) async-start(), calls=%async_computation.13 | async-start | bytes 15728640 | tf_op jit(solution)/shard_map/all_gather | solution.py:16
  126.9 328.6 %copy-start.22 = (f32[768]{0:T(1024)}, f32[768]{0:T(1024)S(1)}, u32[]{:S(2)}) copy-start(f32[768]{0:T(1024)S(1)} %get-tuple-element.111) | copy-start | bytes 9220
  126.9 328.6 %copy-start.24 = (f32[768]{0:T(1024)}, f32[768]{0:T(1024)S(1)}, u32[]{:S(2)}) copy-start(f32[768]{0:T(1024)S(1)} %get-tuple-element.110) | copy-start | bytes 9220
  208.9 3.2 copy-start.7
  215.9 7.5 copy-start.20
  223.3 6.2 copy-start.36
  229.6 370.2 %all-reduce.7.cloned.1.call-start = ((), (), s32[]{:S(2)}) async-start(), calls=%async_computation.7 | async-start | bytes 6291456 | tf_op jit(solution)/shard_map/psum | solution.py:127
  459.3 1.9 copy-start.4
  461.2 7.4 slice-start
  464.3 4.3 copy-start.34
  464.3 4.3 slice-start.1
  468.6 6.0 copy-start.2
  468.7 7.6 copy-start.33
  474.6 1.7 copy-start.35
  480.3 221.2 %reduce-scatter.24.cloned.1.call-start = ((), (), s32[]{:S(2)}) async-start(), calls=%async_computation.16 | async-start | bytes 73728
  481.1 8.6 copy-start.17
  481.1 8.6 copy-start.19
  481.2 240.6 %reduce-scatter.18.cloned.1.call-start = ((), (), s32[]{:S(2)}) async-start(), calls=%async_computation.10 | async-start | bytes 2654208 | tf_op jit(solution)/shard_map/reduce_scatter | solution.py:167
  489.7 234.2 %reduce-scatter.16.cloned.1.call-start = ((), (), s32[]{:S(2)}) async-start(), calls=%async_computation.9 | async-start | bytes 2654208 | tf_op jit(solution)/shard_map/reduce_scatter | solution.py:165
  489.8 109.9 %copy-start.23 = (f32[768]{0:T(1024)S(1)}, f32[768]{0:T(1024)}, u32[]{:S(2)}) copy-start(f32[768]{0:T(1024)} %copy-done.22) | copy-start | bytes 9220
  497.9 109.8 %copy-start.21 = (f32[2048]{0:T(1024)S(1)}, f32[2048]{0:T(1024)}, u32[]{:S(2)}) copy-start(f32[2048]{0:T(1024)} %copy-done.20) | copy-start | bytes 24580
  497.9 228.1 %reduce-scatter.22.cloned.1.call-start = ((), (), s32[]{:S(2)}) async-start(), calls=%async_computation.15 | async-start | bytes 884736
  599.7 8.0 copy-start.5
  613.8 2.6 copy-start.3
  629.9 9.5 %copy-start.13 = (bf16[4,512,1,3,64]{1,0,4,3,2:T(4,128)(2,1)S(1)}, bf16[4,512,1,3,64]{1,0,4,3,2:T(4,128)(2,1)}, u32[]{:S(2)}) copy-start(bf16[4,512,1,3,64]{1,0,4,3,2:T(4,128)(2,1)} %copy-done.12) | copy-start | bytes 2359300
  636.8 2.6 copy-start.1
  669.9 77.4 %reduce-scatter.20.cloned.1.call-start = ((), (), s32[]{:S(2)}) async-start(), calls=%async_computation.14 | async-start | bytes 2211840
  688.3 128.1 %all-reduce.9.cloned.1.call-start = ((), (), s32[]{:S(2)}) async-start(), calls=%async_computation.8 | async-start | bytes 6291456 | tf_op jit(solution)/shard_map/psum | solution.py:158
  689.7 8.3 copy-start.27
  689.7 11.7 %copy-start.25 = (f32[768]{0:T(1024)S(1)}, f32[768]{0:T(1024)}, u32[]{:S(2)}) copy-start(f32[768]{0:T(1024)} %get-tuple-element.104) | copy-start | bytes 9220
  689.7 15.2 %copy-start.26 = (f32[768]{0:T(1024)S(1)}, f32[768]{0:T(1024)}, u32[]{:S(2)}) copy-start(f32[768]{0:T(1024)} %get-tuple-element.107) | copy-start | bytes 9220
  696.0 9.0 %copy-start.10 = (bf16[2048,3,192]{0,2,1:T(8,128)(2,1)S(1)}, bf16[2048,3,192]{0,2,1:T(8,128)(2,1)}, u32[]{:S(2)}) copy-start(bf16[2048,3,192]{0,2,1:T(8,128)(2,1)} %constant_dynamic-update-slice_fusion) | copy-start | bytes 7077892
  696.0 31.0 %copy-start.15 = (f32[3,192,96]{2,1,0:T(8,128)S(1)}, f32[3,192,96]{2,1,0:T(8,128)}, u32[]{:S(2)}) copy-start(f32[3,192,96]{2,1,0:T(8,128)} %param.17) | copy-start | bytes 663556
  696.0 159.9 %reduce-scatter.26.cloned.1.call-start = ((), (), s32[]{:S(2)}) async-start(), calls=%async_computation.17 | async-start | bytes 442368
  702.3 119.6 %copy-start.28 = (f32[6,16]{1,0:T(8,128)}, f32[6,16]{1,0:T(8,128)S(1)}, u32[]{:S(2)}) copy-start(f32[6,16]{1,0:T(8,128)S(1)} %copy.176) | copy-start | bytes 1156
  720.5 101.3 %copy-start.30 = (f32[2,3,8]{2,0,1:T(2,128)}, f32[2,3,8]{2,0,1:T(2,128)S(1)}, u32[]{:S(2)}) copy-start(f32[2,3,8]{2,0,1:T(2,128)S(1)} %get-tuple-element.115) | copy-start | bytes 580
  727.0 94.9 %copy-start.14 = (f32[192,96]{1,0:T(8,128)}, f32[192,96]{1,0:T(8,128)S(1)}, u32[]{:S(2)}) copy-start(f32[192,96]{1,0:T(8,128)S(1)} %copy.174) | copy-start | bytes 221188
  748.5 73.3 %copy-start.31 = (f32[1,768]{1,0:T(1,128)S(1)}, f32[1,768]{1,0:T(1,128)}, u32[]{:S(2)}) copy-start(f32[1,768]{1,0:T(1,128)} %reshape.225) | copy-start | bytes 9220
  748.6 108.2 %copy-start.32 = (f32[3,6,96]{2,1,0:T(8,128)S(1)}, f32[3,6,96]{2,1,0:T(8,128)}, u32[]{:S(2)}) copy-start(f32[3,6,96]{2,1,0:T(8,128)} %param.21) | copy-start | bytes 20740
  856.7 0.6 copy-start.29
Sparse Core Ops, SparseCore 0:
  87.6 121.2 all-reduce.4
  229.7 217.1 all-gather.15
  480.4 119.2 all-reduce.6
  696.1 120.2 all-reduce.8
Sparse Core Ops, SparseCore 1:
  90.4 25.2 all-gather.11
  117.9 23.8 all-gather.13
  484.4 31.7 reduce-scatter.23
  520.1 42.2 reduce-scatter.17
  566.2 42.2 reduce-scatter.15
  670.0 33.9 reduce-scatter.21
  707.2 40.0 reduce-scatter.19
  822.9 32.9 reduce-scatter.25
